TPU v7x, 256 devices: a whole 4x4x8 slice. The times are simulated.
256 devices in a mesh: dp: 2 (over y_hi), fsdp: 16 (over x, y_lo, core), tensor: 8 (over z).
Axes of the slice: x: 4, y: 4 (y_hi: 2, y_lo: 2; y = y_hi * 2 + y_lo), z: 8, core: 2. Of those that a mesh axis runs over, the one named last changes fastest.
Arguments:
- activations: bfloat16 [4096, 8192], P(('dp', 'fsdp'), 'tensor'), may hold values from -6 to 6
- cotangent: bfloat16 [4096, 8192], P(('dp', 'fsdp'), 'tensor'), may hold values from -6 to 6
- up_tiles: bfloat16 [1024, 128, 128], P(('fsdp', 'tensor')), may hold values from -0.1875 to 0.1875
- down_tiles: bfloat16 [1024, 128, 128], P(('fsdp', 'tensor')), may hold values from -0.125 to 0.125
- up_rows: int32 [128, 8], P(None, 'tensor'), may hold values from 0 to 63, as said below
- up_cols: int32 [128, 8], P(None, 'tensor'), may hold values from 0 to 15, as said below
- down_rows: int32 [128, 8], P(None, 'tensor'), may hold values from 0 to 15, as said below
- down_cols: int32 [128, 8], P(None, 'tensor'), may hold values from 0 to 63, as said below
Outputs:
- output: bfloat16 [4096, 8192], P(('dp', 'fsdp'), 'tensor')
- input_grad: bfloat16 [4096, 8192], P(('dp', 'fsdp'), 'tensor')
- up_grad: float32 [1024, 128, 128], P(('fsdp', 'tensor'))
- down_grad: float32 [1024, 128, 128], P(('fsdp', 'tensor'))
Inputs may be any that keep to these rules, and one draw needn't show every extreme that they name: `up_rows`: within a column, the up tiles of one hidden-unit block name distinct feature blocks. `up_cols`: every value occurs exactly 8 times in each column. `down_rows`: every value occurs exactly 8 times in each column. `down_cols`: within a column, the down tiles of one hidden-unit block name distinct feature blocks.
All inputs are finite; a program needn't handle non-finite values.
Results may differ from a plain program's by a relative error of at most 0.018.
Values may be sent and summed in bfloat16 or wider, within the bound.
No kernel may reach another device: no remote copies, remote signals or barrier semaphores. Data moves between devices by JAX's collectives and lax.ppermute only.
A program may use at most 128 MiB of HBM per device.

v0:
```python
import jax
import jax.numpy as jnp
from jax import lax
from jax.sharding import PartitionSpec as P

D = 8192
FF = 16384
inv_root_two = 0.7071067811865476
inv_root_tau = 0.3989422804014327


def gelu_parts(values):
    normal_cdf = 0.5 * (1.0 + jax.scipy.special.erf(values * inv_root_two))
    density = inv_root_tau * jnp.exp(-0.5 * values * values)
    return (values * normal_cdf, normal_cdf + values * density)


def grouped_pick(acting, far_index, hidden_blocks, block_size):
    rows_here = acting.shape[0]
    picked = acting.reshape(rows_here, -1, block_size)[:, far_index]
    return picked.reshape(rows_here, hidden_blocks, -1, block_size)


def add_far(product, far_index, model_blocks):
    rows_here = product.shape[0]
    block_size = product.shape[-1]
    flat = product.reshape(rows_here, -1, block_size)
    summed = (
        jnp.zeros((rows_here, model_blocks, block_size), jnp.float32).at[:, far_index].add(flat)
    )
    return summed.reshape(rows_here, model_blocks * block_size)


def grouped_tiles(tiles, order, hidden_blocks):
    block_size = tiles.shape[1]
    return tiles[order].reshape(hidden_blocks, -1, block_size, block_size)


def body(activations, cotangent, up_tiles, down_tiles, up_rows, up_cols, down_rows, down_cols):
    block_size = up_tiles.shape[1]
    hidden_blocks = FF // (block_size * lax.axis_size("tensor"))
    model_blocks = D // block_size
    up_order = jnp.argsort(up_cols[:, 0], stable=True)
    down_order = jnp.argsort(down_rows[:, 0], stable=True)
    up_back = jnp.argsort(up_order)
    down_back = jnp.argsort(down_order)
    up_far = up_rows[:, 0][up_order]
    down_far = down_cols[:, 0][down_order]
    full_input = lax.all_gather(activations, "tensor", axis=1, tiled=True)
    input_pick = grouped_pick(full_input, up_far, hidden_blocks, block_size)
    up_whole = lax.all_gather(up_tiles, "fsdp", axis=0, tiled=True)
    up_sorted = grouped_tiles(up_whole, up_order, hidden_blocks)
    pre_act = jnp.einsum(
        "thkb,hkbc->thc", input_pick, up_sorted, preferred_element_type=jnp.float32
    )
    gelu_out, gelu_slope = gelu_parts(pre_act)
    hidden = gelu_out.astype(jnp.bfloat16)
    down_whole = lax.all_gather(down_tiles, "fsdp", axis=0, tiled=True)
    down_sorted = grouped_tiles(down_whole, down_order, hidden_blocks)
    out_product = jnp.einsum(
        "thb,hkbc->thkc", hidden, down_sorted, preferred_element_type=jnp.float32
    )
    partial_out = add_far(out_product, down_far, model_blocks)
    output = lax.psum_scatter(
        partial_out.astype(jnp.bfloat16), "tensor", scatter_dimension=1, tiled=True
    )
    full_cotangent = lax.all_gather(cotangent, "tensor", axis=1, tiled=True)
    cot_pick = grouped_pick(full_cotangent, down_far, hidden_blocks, block_size)
    hidden_grad = jnp.einsum(
        "thkc,hkbc->thb", cot_pick, down_sorted, preferred_element_type=jnp.float32
    )
    pre_grad = (hidden_grad * gelu_slope).astype(jnp.bfloat16)
    in_product = jnp.einsum(
        "thc,hkbc->thkb", pre_grad, up_sorted, preferred_element_type=jnp.float32
    )
    partial_in = add_far(in_product, up_far, model_blocks)
    input_grad = lax.psum_scatter(
        partial_in.astype(jnp.bfloat16), "tensor", scatter_dimension=1, tiled=True
    )
    up_grouped = jnp.einsum(
        "thkb,thc->hkbc", input_pick, pre_grad, preferred_element_type=jnp.float32
    )
    down_grouped = jnp.einsum(
        "thb,thkc->hkbc", hidden, cot_pick, preferred_element_type=jnp.float32
    )
    up_rounded = up_grouped.astype(jnp.bfloat16).reshape(-1, block_size, block_size)
    down_rounded = down_grouped.astype(jnp.bfloat16).reshape(-1, block_size, block_size)
    up_term = up_rounded[up_back].astype(jnp.float32)
    down_term = down_rounded[down_back].astype(jnp.float32)
    up_part, down_part = (
        lax.psum_scatter(
            up_term.astype(jnp.bfloat16), "fsdp", scatter_dimension=0, tiled=True
        ).astype(jnp.float32),
        lax.psum_scatter(
            down_term.astype(jnp.bfloat16), "fsdp", scatter_dimension=0, tiled=True
        ).astype(jnp.float32),
    )
    up_grad, down_grad = (
        lax.psum(up_part.astype(jnp.bfloat16), "dp").astype(jnp.float32),
        lax.psum(down_part.astype(jnp.bfloat16), "dp").astype(jnp.float32),
    )
    return (output, input_grad, up_grad, down_grad)


def solution(mesh):
    in_specs = (
        P(("dp", "fsdp"), "tensor"),
        P(("dp", "fsdp"), "tensor"),
        P(("fsdp", "tensor"), None, None),
        P(("fsdp", "tensor"), None, None),
        P(None, "tensor"),
        P(None, "tensor"),
        P(None, "tensor"),
        P(None, "tensor"),
    )
    out_specs = (
        P(("dp", "fsdp"), "tensor"),
        P(("dp", "fsdp"), "tensor"),
        P(("fsdp", "tensor"), None, None),
        P(("fsdp", "tensor"), None, None),
    )
    return jax.shard_map(body, mesh=mesh, in_specs=in_specs, out_specs=out_specs, check_vma=False)
```

profile of v0, /device:TPU:1, one launch (start us, length us, event | category | flops | bytes accessed | tf_op | source)
XLA Modules:
  0.0 480.6 jit_solution(9236470539080875752)
XLA Ops:
  12.3 3.2 sort.63
  19.3 3.2 sort.62
  24.1 28.0 %all-gather.9.cloned.1.call-done = bf16[128,8192]{0,1:T(8,128)(2,1)} async-done(((bf16[128,1024]{0,1:T(8,128)(2,1)}), bf16[128,8192]{0,1:T(8,128)(2,1)}) %all-gather.9.cloned.1.call-update) | async-done | bytes 2097168 | tf_op jit(solution)/shard_map/all_gather | solution.py:49
  52.1 3.2 copy.59
  55.3 39.0 %all-gather.11.cloned.1.call-done = bf16[128,8192]{0,1:T(8,128)(2,1)} async-done(((bf16[128,1024]{0,1:T(8,128)(2,1)}), bf16[128,8192]{0,1:T(8,128)(2,1)}) %all-gather.11.cloned.1.call-update) | async-done | bytes 2097168 | tf_op jit(solution)/shard_map/all_gather | solution.py:67
  94.3 4.1 copy.66
  98.4 3.0 gather_fusion.4
  101.4 4.6 gather_fusion.5
  106.0 32.7 %all-gather.7.cloned.1.call-done = bf16[128,128,128]{2,1,0:T(8,128)(2,1)} async-done(((bf16[8,128,128]{2,1,0:T(8,128)(2,1)}), bf16[128,128,128]{2,1,0:T(8,128)(2,1)}) %all-gather.7.cloned.1.call-update) | async-done | bytes 4194320 | tf_op jit(solution)/shard_map/all_gather | solution.py:51
  138.7 5.2 %gather_fusion.2 = bf16[128,128,128]{2,1,0:T(8,128)(2,1)} fusion(bf16[128,128,128]{2,1,0:T(8,128)(2,1)} %all-gather.7.cloned.1.call-done, s32[1024]{0:T(1024)S(1)} %pad_clamp_fusion.4), kind=kCustom, calls=%fused_computation.2 | custom fusion | bytes 8389120 | tf_op jit(solution)/shard_map/gather | solution.py:36
  143.9 4.8 convolution_bitcast_fusion.1
  148.7 31.7 %all-gather.5.cloned.1.call-done = bf16[128,128,128]{2,1,0:T(8,128)(2,1)} async-done(((bf16[8,128,128]{2,1,0:T(8,128)(2,1)}), bf16[128,128,128]{2,1,0:T(8,128)(2,1)}) %all-gather.5.cloned.1.call-update) | async-done | bytes 4194320 | tf_op jit(solution)/shard_map/all_gather | solution.py:58
  180.5 5.2 %gather_fusion.1 = bf16[128,128,128]{2,1,0:T(8,128)(2,1)} fusion(bf16[128,128,128]{2,1,0:T(8,128)(2,1)} %all-gather.5.cloned.1.call-done, s32[1024]{0:T(1024)S(1)} %pad_clamp_fusion.5), kind=kCustom, calls=%fused_computation.1 | custom fusion | bytes 8389120 | tf_op jit(solution)/shard_map/gather | solution.py:36
  185.7 5.0 %fusion.2 = bf16[128,16,128,1]{0,2,3,1:T(8,128)(2,1)S(1)} fusion(bf16[16,8,128,128]{3,2,1,0:T(8,128)(2,1)} %bitcast.84, bf16[128,16,8,128]{3,0,2,1:T(8,128)(2,1)} %bitcast.86, f32[128,16,128]{0,2,1:T(8,128)S(1)} %convolution_bitcast_fusion.1), kind=kOutput, calls=%fused_computation.17 | convolution fusion | flops 539492352 | bytes 9961472 | tf_op jit(solution)/shard_map/thkc,hkbc->thb/dot_general | solution.py:69
  190.7 3.3 convolution_convert_fusion.1
  194.0 5.2 %gather_fusion.6 = bf16[128,128,128]{2,1,0:T(8,128)(2,1)} fusion(bf16[128,128,128]{2,1,0:T(8,128)(2,1)} %bitcast.88, s32[1024]{0:T(1024)S(1)} %pad_clamp_fusion.1), kind=kCustom, calls=%fused_computation.6 | custom fusion | bytes 8389120 | tf_op jit(solution)/shard_map/gather | solution.py:88
  202.0 5.6 %convolution_convert_fusion = bf16[16,8,128,128]{3,2,1,0:T(8,128)(2,1)} fusion(bf16[128,16,8,128]{3,0,2,1:T(8,128)(2,1)} %bitcast.87, f32[128,16,128]{0,2,1:T(8,128)S(1)} %convolution_bitcast_fusion.1), kind=kOutput, calls=%fused_computation.10 | convolution fusion | flops 540278784 | bytes 9437184 | tf_op jit(solution)/shard_map/thb,thkc->hkbc/dot_general | solution.py:83
  207.6 6.4 %copy.74 = bf16[128,128,128]{2,1,0:T(8,128)(2,1)} copy(bf16[128,128,128]{1,2,0:T(8,128)(2,1)} %bitcast.89) | data formatting | bytes 8388608 | tf_op jit(solution)/shard_map/reshape | solution.py:87
  214.0 5.3 %gather_fusion.7 = bf16[128,128,128]{2,1,0:T(8,128)(2,1)} fusion(bf16[128,128,128]{2,1,0:T(8,128)(2,1)} %copy.74, s32[1024]{0:T(1024)S(1)} %pad_clamp_fusion), kind=kCustom, calls=%fused_computation.7 | custom fusion | bytes 8389120 | tf_op jit(solution)/shard_map/gather | solution.py:89
  219.4 6.7 %fusion.13 = f32[16,8,128,128]{3,2,1,0:T(8,128)} fusion(bf16[16,8,128,128]{3,2,1,0:T(8,128)(2,1)} %bitcast.77, bf16[128,16,128,1]{0,2,3,1:T(8,128)(2,1)S(1)} %fusion.2), kind=kOutput, calls=%fused_computation.40 | convolution fusion | flops 536870912 | bytes 13107200 | tf_op jit(solution)/shard_map/thc,hkbc->thkb/dot_general | solution.py:73
  226.1 9.0 %copy.68 = f32[128,128,128]{2,0,1:T(8,128)} copy(f32[128,128,128]{0,2,1:T(8,128)} %bitcast.82) | data formatting | bytes 16777216 | tf_op jit(solution)/shard_map/reshape | solution.py:27
  237.6 26.7 %scatter_fusion.1 = f32[128,64,128]{2,0,1:T(8,128)} fusion(f32[128,64,128]{2,0,1:T(8,128)} %broadcast.42.clone.1, s32[128]{0:T(128)S(1)} %fusion.9, f32[128,128,128]{2,1,0:T(8,128)} %bitcast.81), kind=kCustom, calls=%fused_computation.9 | custom fusion | flops 2097152 | bytes 25166336 | tf_op jit(solution)/shard_map/scatter-add | solution.py:29
  264.3 2.6 convert_element_type.45
  266.9 2.9 copy.69
  270.0 6.8 %fusion.11 = f32[16,8,128,128]{3,2,1,0:T(8,128)} fusion(bf16[16,8,128,128]{3,2,1,0:T(8,128)(2,1)} %bitcast.85, f32[128,16,128]{0,2,1:T(8,128)S(1)} %convolution_bitcast_fusion.1), kind=kOutput, calls=%fused_computation.39 | convolution fusion | flops 538181632 | bytes 13631488 | tf_op jit(solution)/shard_map/thb,hkbc->thkc/dot_general | solution.py:60
  276.7 9.0 %copy.63 = f32[128,128,128]{2,0,1:T(8,128)} copy(f32[128,128,128]{0,2,1:T(8,128)} %bitcast.83) | data formatting | bytes 16777216 | tf_op jit(solution)/shard_map/reshape | solution.py:27
  288.2 26.9 %scatter_fusion = f32[128,64,128]{2,0,1:T(8,128)} fusion(f32[128,64,128]{2,0,1:T(8,128)} %broadcast.42.clone, s32[128]{0:T(128)S(1)} %fusion.8, f32[128,128,128]{2,1,0:T(8,128)} %bitcast.80), kind=kCustom, calls=%fused_computation.8 | custom fusion | flops 2097152 | bytes 25166336 | tf_op jit(solution)/shard_map/scatter-add | solution.py:29
  317.7 2.9 copy.64
  320.7 16.4 %reduce-scatter.11.cloned.1.call-done = bf16[8,128,128]{2,1,0:T(8,128)(2,1)} async-done(((bf16[128,128,128]{2,1,0:T(8,128)(2,1)}), bf16[8,128,128]{2,1,0:T(8,128)(2,1)}) %reduce-scatter.11.cloned.1.call-update) | async-done | bytes 262160 | tf_op jit(solution)/shard_map/reduce_scatter | solution.py:94
  337.1 42.2 %reduce-scatter.7.cloned.1.call-done = bf16[128,1024]{0,1:T(8,128)(2,1)} async-done(((bf16[128,8192]{0,1:T(8,128)(2,1)}), bf16[128,1024]{0,1:T(8,128)(2,1)}) %reduce-scatter.7.cloned.1.call-update) | async-done | bytes 262160 | tf_op jit(solution)/shard_map/reduce_scatter | solution.py:77
  381.1 41.9 %reduce-scatter.5.cloned.1.call-done = bf16[128,1024]{0,1:T(8,128)(2,1)} async-done(((bf16[128,8192]{0,1:T(8,128)(2,1)}), bf16[128,1024]{0,1:T(8,128)(2,1)}) %reduce-scatter.5.cloned.1.call-update) | async-done | bytes 262160 | tf_op jit(solution)/shard_map/reduce_scatter | solution.py:64
  424.8 45.7 %all-reduce.3.cloned.1.call-done = (bf16[8,128,128]{2,1,0:T(8,128)(2,1)}, bf16[8,128,128]{2,1,0:T(8,128)(2,1)}) async-done(((bf16[8,128,128]{2,1,0:T(8,128)(2,1)}, bf16[8,128,128]{2,1,0:T(8,128)(2,1)}), (bf16[8,128,128]{2,1,0:T(8,128)(2,1)}, bf16[8,128,128]{2,1,0:T(8,128)(2,1)})) %all-reduce.3.cloned.1.call-update) | async-done | bytes 524304 | tf_op jit(solution)/shard_map/psum | solution.py:99
  (54 shorter events, 28.1 us)
Async XLA Ops:
  7.2 10.9 %copy-start = (s32[128,1]{0,1:T(1,128)S(1)}, s32[128,1]{0,1:T(1,128)}, u32[]{:S(2)}) copy-start(s32[128,1]{0,1:T(1,128)} %param.12) | copy-start | bytes 1540
  7.2 44.9 %all-gather.9.cloned.1.call-start = ((), (), s32[]{:S(2)}) async-start(), calls=%async_computation.6 | async-start | bytes 2359296 | tf_op jit(solution)/shard_map/all_gather | solution.py:49
  9.0 85.3 %all-gather.11.cloned.1.call-start = ((), (), s32[]{:S(2)}) async-start(), calls=%async_computation.8 | async-start | bytes 2359296 | tf_op jit(solution)/shard_map/all_gather | solution.py:67
  10.9 127.8 %all-gather.7.cloned.1.call-start = ((), (), s32[]{:S(2)}) async-start(), calls=%async_computation.5 | async-start | bytes 4456448 | tf_op jit(solution)/shard_map/all_gather | solution.py:51
  11.7 168.8 %all-gather.5.cloned.1.call-start = ((), (), s32[]{:S(2)}) async-start(), calls=%async_computation.4 | async-start | bytes 4456448 | tf_op jit(solution)/shard_map/all_gather | solution.py:58
  12.2 308.5 %reduce-scatter.9.cloned.1.call-start = ((), (), s32[]{:S(2)}) async-start(), calls=%async_computation.10 | async-start | bytes 4456448 | tf_op jit(solution)/shard_map/reduce_scatter | solution.py:91
  185.7 5.0 %copy-start.2 = (bf16[128,128,128]{2,1,0:T(8,128)(2,1)S(1)}, bf16[128,128,128]{2,1,0:T(8,128)(2,1)}, u32[]{:S(2)}) copy-start(bf16[128,128,128]{2,1,0:T(8,128)(2,1)} %gather_fusion.4) | copy-start | bytes 12582916
  199.2 137.9 %reduce-scatter.11.cloned.1.call-start = ((), (), s32[]{:S(2)}) async-start(), calls=%async_computation.11 | async-start | bytes 4456448 | tf_op jit(solution)/shard_map/reduce_scatter | solution.py:94
  219.4 160.0 %reduce-scatter.7.cloned.1.call-start = ((), (), s32[]{:S(2)}) async-start(), calls=%async_computation.9 | async-start | bytes 2359296 | tf_op jit(solution)/shard_map/reduce_scatter | solution.py:77
  269.9 153.1 %reduce-scatter.5.cloned.1.call-start = ((), (), s32[]{:S(2)}) async-start(), calls=%async_computation.7 | async-start | bytes 2359296 | tf_op jit(solution)/shard_map/reduce_scatter | solution.py:64
  315.1 158.9 %copy-start.1 = (s32[128,1]{0,1:T(1,128)S(1)}, s32[128,1]{0,1:T(1,128)}, u32[]{:S(2)}) copy-start(s32[128,1]{0,1:T(1,128)} %param.12) | copy-start | bytes 1540
  320.7 149.9 %all-reduce.3.cloned.1.call-start = ((), (), s32[]{:S(2)}) async-start(), calls=%async_computation.12 | async-start | bytes 1048576 | tf_op jit(solution)/shard_map/psum | solution.py:99
Sparse Core Ops, SparseCore 0:
  10.4 41.6 all-gather.8
  54.5 39.8 all-gather.10
  96.2 42.5 all-gather.6
  140.4 39.9 all-gather.4
  199.3 66.5 reduce-scatter.8
  268.4 68.6 reduce-scatter.10
  339.7 39.6 reduce-scatter.6
  381.9 41.0 reduce-scatter.4
  425.7 44.8 all-reduce.2
where the time goes:
time: 482 us; the launch traced here: 481 us
  waiting for transfers between devices  279 us (58%)
  local copies, waits for them, and re-layouts  81.1 us (17%)
  other arithmetic  73.8 us (15%)
  matrix products  32.2 us (7%)
  between operations  14 us (3%)
    scatter-add x2, other arithmetic, add_far(): jnp.zeros((rows_here, model_blocks, block_size), jnp.float32)  53.6 us
    psum x1, waiting for transfers between devices, body(): lax.psum(up_part.astype(jnp.bfloat16), 'dp').astype(jnp.float32)  45.7 us
    reduce_scatter x1, waiting for transfers between devices, body(): lax.psum_scatter(partial_in.astype(jnp.bfloat16), 'tensor', scatter_dimen...  42.2 us
    reduce_scatter x1, waiting for transfers between devices, body(): lax.psum_scatter(partial_out.astype(jnp.bfloat16), 'tensor', scatter_dime...  41.9 us
    all_gather x1, waiting for transfers between devices, body(): full_cotangent = lax.all_gather(cotangent, 'tensor', axis=1, tiled=True)  39 us
    all_gather x1, waiting for transfers between devices, body(): up_whole = lax.all_gather(up_tiles, 'fsdp', axis=0, tiled=True)  32.7 us
    all_gather x1, waiting for transfers between devices, body(): down_whole = lax.all_gather(down_tiles, 'fsdp', axis=0, tiled=True)  31.7 us
    all_gather x1, waiting for transfers between devices, body(): full_input = lax.all_gather(activations, 'tensor', axis=1, tiled=True)  28 us
  transfers between devices with their start and end apart: 9, of which 8 were waited for; matrix products, arithmetic and copies ran while one was open for 34% of the time, Pallas kernels for 0%

commit v1 on v0

--- a/solution.py
+++ b/solution.py
@@ -64,7 +64,15 @@
     output = lax.psum_scatter(
         partial_out.astype(jnp.bfloat16), "tensor", scatter_dimension=1, tiled=True
     )
-    full_cotangent = lax.all_gather(cotangent, "tensor", axis=1, tiled=True)
+    count = lax.axis_size("tensor")
+    held, parts = (cotangent, [cotangent])
+    for _ in range(count - 1):
+        held = lax.ppermute(held, "tensor", [(i, (i + 1) % count) for i in range(count)])
+        parts.insert(0, held)
+    row_of_blocks = jnp.concatenate(parts, axis=1)
+    full_cotangent = jnp.roll(
+        row_of_blocks, (lax.axis_index("tensor") + 1) * cotangent.shape[1], axis=1
+    )
     cot_pick = grouped_pick(full_cotangent, down_far, hidden_blocks, block_size)
     hidden_grad = jnp.einsum(
         "thkc,hkbc->thb", cot_pick, down_sorted, preferred_element_type=jnp.float32

time: 482 us -> 450 us (0.934)
  waiting for transfers between devices: 279 us -> 244 us
    ppermute x0 -> x7, waiting for transfers between devices: none -> 55.5 us  [body(): lax.ppermute(held, 'tensor', [(i, (i + 1) % count) for i in range(count)])]
    all_gather x1 -> x0, waiting for transfers between devices: 39 us -> none  [body(): full_cotangent = lax.all_gather(cotangent, 'tensor', axis=1, tiled=True)]
    all_gather x1, waiting for transfers between devices: 28 us -> 0.01 us  [body(): full_input = lax.all_gather(activations, 'tensor', axis=1, tiled=True)]
    all_gather x1, waiting for transfers between devices: 32.7 us -> 6.58 us  [body(): up_whole = lax.all_gather(up_tiles, 'fsdp', axis=0, tiled=True)]
  transfers between devices with their start and end apart: 9 -> 15, of which waited for: 8 -> 13; matrix products, arithmetic and copies ran while one was open for 34% -> 36% of each run, Pallas kernels for 0% -> 0%
where the time goes in v1:
time: 450 us; the launch traced here: 448 us
  waiting for transfers between devices  244 us (54%)
  local copies, waits for them, and re-layouts  80 us (18%)
  other arithmetic  73.9 us (16%)
  matrix products  32.2 us (7%)
  between operations  14.4 us (3%)
    ppermute x7, waiting for transfers between devices, body(): lax.ppermute(held, 'tensor', [(i, (i + 1) % count) for i in range(count)])  55.5 us
    scatter-add x2, other arithmetic, add_far(): jnp.zeros((rows_here, model_blocks, block_size), jnp.float32)  53.6 us
    psum x1, waiting for transfers between devices, body(): lax.psum(up_part.astype(jnp.bfloat16), 'dp').astype(jnp.float32)  45.8 us
    reduce_scatter x1, waiting for transfers between devices, body(): lax.psum_scatter(partial_in.astype(jnp.bfloat16), 'tensor', scatter_dimen...  41.9 us
    reduce_scatter x1, waiting for transfers between devices, body(): lax.psum_scatter(partial_out.astype(jnp.bfloat16), 'tensor', scatter_dime...  41.9 us
    all_gather x1, waiting for transfers between devices, body(): down_whole = lax.all_gather(down_tiles, 'fsdp', axis=0, tiled=True)  31.9 us
    reduce_scatter x1, waiting for transfers between devices, body(): lax.psum_scatter(down_term.astype(jnp.bfloat16), 'fsdp', scatter_dimensio...  18.9 us
    reshape x2, local copies, waits for them, and re-layouts, add_far(): flat = product.reshape(rows_here, -1, block_size)  18 us
  transfers between devices with their start and end apart: 15, of which 13 were waited for; matrix products, arithmetic and copies ran while one was open for 36% of the time, Pallas kernels for 0%

profile of v1, /device:TPU:1, one launch (start us, length us, event | category | flops | bytes accessed | tf_op | source)
XLA Modules:
  0.0 448.1 jit_solution(10460431761399955219)
XLA Ops:
  14.2 10.0 %collective-permute-done = bf16[128,1024]{0,1:T(8,128)(2,1)S(1)} collective-permute-done((bf16[128,1024]{0,1:T(8,128)(2,1)S(1)}, bf16[128,1024]{0,1:T(8,128)(2,1)S(1)}, u32[]{:S(2)}, u32[]{:S(2)}) %collective-permute-start) | collective-permute-done | bytes 262176 | tf_op jit(solution)/shard_map/ppermute | solution.py:70
  24.2 3.2 sort.62
  27.4 6.6 %collective-permute-done.1 = bf16[128,1024]{0,1:T(8,128)(2,1)S(1)} collective-permute-done((bf16[128,1024]{0,1:T(8,128)(2,1)S(1)}, bf16[128,1024]{0,1:T(8,128)(2,1)S(1)}, u32[]{:S(2)}, u32[]{:S(2)}) %collective-permute-start.1) | collective-permute-done | bytes 262176 | tf_op jit(solution)/shard_map/ppermute | solution.py:70
  35.8 11.1 %collective-permute-done.2 = bf16[128,1024]{0,1:T(8,128)(2,1)S(1)} collective-permute-done((bf16[128,1024]{0,1:T(8,128)(2,1)S(1)}, bf16[128,1024]{0,1:T(8,128)(2,1)S(1)}, u32[]{:S(2)}, u32[]{:S(2)}) %collective-permute-start.2) | collective-permute-done | bytes 262176 | tf_op jit(solution)/shard_map/ppermute | solution.py:70
  47.0 3.2 sort.63
  50.2 10.0 %collective-permute-done.3 = bf16[128,1024]{0,1:T(8,128)(2,1)S(1)} collective-permute-done((bf16[128,1024]{0,1:T(8,128)(2,1)S(1)}, bf16[128,1024]{0,1:T(8,128)(2,1)S(1)}, u32[]{:S(2)}, u32[]{:S(2)}) %collective-permute-start.3) | collective-permute-done | bytes 262176 | tf_op jit(solution)/shard_map/ppermute | solution.py:70
  69.7 5.5 %collective-permute-done.5 = bf16[128,1024]{0,1:T(8,128)(2,1)S(1)} collective-permute-done((bf16[128,1024]{0,1:T(8,128)(2,1)S(1)}, bf16[128,1024]{0,1:T(8,128)(2,1)S(1)}, u32[]{:S(2)}, u32[]{:S(2)}) %collective-permute-start.5) | collective-permute-done | bytes 262176 | tf_op jit(solution)/shard_map/ppermute | solution.py:70
  75.3 9.4 %collective-permute-done.6 = bf16[128,1024]{0,1:T(8,128)(2,1)S(1)} collective-permute-done((bf16[128,1024]{0,1:T(8,128)(2,1)S(1)}, bf16[128,1024]{0,1:T(8,128)(2,1)S(1)}, u32[]{:S(2)}, u32[]{:S(2)}) %collective-permute-start.6) | collective-permute-done | bytes 262176 | tf_op jit(solution)/shard_map/ppermute | solution.py:70
  86.8 3.3 copy.69
  90.1 3.1 gather_fusion.5
  93.1 3.3 copy.60
  99.4 6.6 %all-gather.6.cloned.1.call-done = bf16[128,128,128]{2,1,0:T(8,128)(2,1)} async-done(((bf16[8,128,128]{2,1,0:T(8,128)(2,1)}), bf16[128,128,128]{2,1,0:T(8,128)(2,1)}) %all-gather.6.cloned.1.call-update) | async-done | bytes 4194320 | tf_op jit(solution)/shard_map/all_gather | solution.py:51
  106.0 5.2 %gather_fusion.2 = bf16[128,128,128]{2,1,0:T(8,128)(2,1)} fusion(bf16[128,128,128]{2,1,0:T(8,128)(2,1)} %all-gather.6.cloned.1.call-done, s32[1024]{0:T(1024)S(1)} %pad_clamp_fusion.4), kind=kCustom, calls=%fused_computation.2 | custom fusion | bytes 8389120 | tf_op jit(solution)/shard_map/gather | solution.py:36
  111.2 4.8 %convolution_bitcast_fusion.1 = f32[128,16,128]{0,2,1:T(8,128)S(1)} fusion(bf16[16,8,128,128]{3,2,1,0:T(8,128)(2,1)} %bitcast.76, bf16[128,16,8,128]{3,0,2,1:T(8,128)(2,1)} %bitcast.78), kind=kOutput, calls=%fused_computation.14 | convolution fusion | flops 536870912 | bytes 9437184 | tf_op jit(solution)/shard_map/thkb,hkbc->thc/dot_general | solution.py:53
  116.0 31.9 %all-gather.4.cloned.1.call-done = bf16[128,128,128]{2,1,0:T(8,128)(2,1)} async-done(((bf16[8,128,128]{2,1,0:T(8,128)(2,1)}), bf16[128,128,128]{2,1,0:T(8,128)(2,1)}) %all-gather.4.cloned.1.call-update) | async-done | bytes 4194320 | tf_op jit(solution)/shard_map/all_gather | solution.py:58
  147.8 5.2 %gather_fusion.1 = bf16[128,128,128]{2,1,0:T(8,128)(2,1)} fusion(bf16[128,128,128]{2,1,0:T(8,128)(2,1)} %all-gather.4.cloned.1.call-done, s32[1024]{0:T(1024)S(1)} %pad_clamp_fusion.5), kind=kCustom, calls=%fused_computation.1 | custom fusion | bytes 8389120 | tf_op jit(solution)/shard_map/gather | solution.py:36
  153.1 5.0 %fusion.2 = bf16[128,16,128,1]{0,2,3,1:T(8,128)(2,1)S(1)} fusion(bf16[16,8,128,128]{3,2,1,0:T(8,128)(2,1)} %bitcast.84, bf16[128,16,8,128]{3,0,2,1:T(8,128)(2,1)} %bitcast.86, f32[128,16,128]{0,2,1:T(8,128)S(1)} %convolution_bitcast_fusion.1), kind=kOutput, calls=%fused_computation.17 | convolution fusion | flops 539492352 | bytes 9961472 | tf_op jit(solution)/shard_map/thkc,hkbc->thb/dot_general | solution.py:77
  158.0 3.3 convolution_convert_fusion.1
  161.4 5.2 %gather_fusion.6 = bf16[128,128,128]{2,1,0:T(8,128)(2,1)} fusion(bf16[128,128,128]{2,1,0:T(8,128)(2,1)} %bitcast.88, s32[1024]{0:T(1024)S(1)} %get-tuple-element.27), kind=kCustom, calls=%fused_computation.6 | custom fusion | bytes 8389120 | tf_op jit(solution)/shard_map/gather | solution.py:96
  166.7 5.6 %convolution_convert_fusion = bf16[16,8,128,128]{3,2,1,0:T(8,128)(2,1)} fusion(bf16[128,16,8,128]{3,0,2,1:T(8,128)(2,1)} %bitcast.87, f32[128,16,128]{0,2,1:T(8,128)S(1)} %convolution_bitcast_fusion.1), kind=kOutput, calls=%fused_computation.10 | convolution fusion | flops 540278784 | bytes 9437184 | tf_op jit(solution)/shard_map/thb,thkc->hkbc/dot_general | solution.py:91
  172.3 6.4 %copy.77 = bf16[128,128,128]{2,1,0:T(8,128)(2,1)} copy(bf16[128,128,128]{1,2,0:T(8,128)(2,1)} %bitcast.89) | data formatting | bytes 8388608 | tf_op jit(solution)/shard_map/reshape | solution.py:95
  178.7 5.2 %gather_fusion.7 = bf16[128,128,128]{2,1,0:T(8,128)(2,1)} fusion(bf16[128,128,128]{2,1,0:T(8,128)(2,1)} %copy.77, s32[1024]{0:T(1024)S(1)} %get-tuple-element.26), kind=kCustom, calls=%fused_computation.7 | custom fusion | bytes 8389120 | tf_op jit(solution)/shard_map/gather | solution.py:97
  184.2 6.7 %fusion.13 = f32[16,8,128,128]{3,2,1,0:T(8,128)} fusion(bf16[16,8,128,128]{3,2,1,0:T(8,128)(2,1)} %bitcast.77, bf16[128,16,128,1]{0,2,3,1:T(8,128)(2,1)S(1)} %fusion.2), kind=kOutput, calls=%fused_computation.57 | convolution fusion | flops 536870912 | bytes 13107200 | tf_op jit(solution)/shard_map/thc,hkbc->thkb/dot_general | solution.py:81
  190.9 9.0 %copy.71 = f32[128,128,128]{2,0,1:T(8,128)} copy(f32[128,128,128]{0,2,1:T(8,128)} %bitcast.82) | data formatting | bytes 16777216 | tf_op jit(solution)/shard_map/reshape | solution.py:27
  202.4 26.7 %scatter_fusion.1 = f32[128,64,128]{2,0,1:T(8,128)} fusion(f32[128,64,128]{2,0,1:T(8,128)} %broadcast.43.clone.1, s32[128]{0:T(128)S(1)} %fusion.9, f32[128,128,128]{2,1,0:T(8,128)} %bitcast.81), kind=kCustom, calls=%fused_computation.9 | custom fusion | flops 2097152 | bytes 25166336 | tf_op jit(solution)/shard_map/scatter-add | solution.py:29
  234.7 6.8 %fusion.11 = f32[16,8,128,128]{3,2,1,0:T(8,128)} fusion(bf16[16,8,128,128]{3,2,1,0:T(8,128)(2,1)} %bitcast.85, f32[128,16,128]{0,2,1:T(8,128)S(1)} %convolution_bitcast_fusion.1), kind=kOutput, calls=%fused_computation.56 | convolution fusion | flops 538181632 | bytes 13631488 | tf_op jit(solution)/shard_map/thb,hkbc->thkc/dot_general | solution.py:60
  241.5 9.0 %copy.64 = f32[128,128,128]{2,0,1:T(8,128)} copy(f32[128,128,128]{0,2,1:T(8,128)} %bitcast.83) | data formatting | bytes 16777216 | tf_op jit(solution)/shard_map/reshape | solution.py:27
  253.0 26.9 %scatter_fusion = f32[128,64,128]{2,0,1:T(8,128)} fusion(f32[128,64,128]{2,0,1:T(8,128)} %broadcast.43.clone, s32[128]{0:T(128)S(1)} %fusion.8, f32[128,128,128]{2,1,0:T(8,128)} %bitcast.80), kind=kCustom, calls=%fused_computation.8 | custom fusion | flops 2097152 | bytes 25166336 | tf_op jit(solution)/shard_map/scatter-add | solution.py:29
  285.6 18.9 %reduce-scatter.11.cloned.1.call-done = bf16[8,128,128]{2,1,0:T(8,128)(2,1)} async-done(((bf16[128,128,128]{2,1,0:T(8,128)(2,1)}), bf16[8,128,128]{2,1,0:T(8,128)(2,1)}) %reduce-scatter.11.cloned.1.call-update) | async-done | bytes 262160 | tf_op jit(solution)/shard_map/reduce_scatter | solution.py:102
  304.5 41.9 %reduce-scatter.7.cloned.1.call-done = bf16[128,1024]{0,1:T(8,128)(2,1)} async-done(((bf16[128,8192]{0,1:T(8,128)(2,1)}), bf16[128,1024]{0,1:T(8,128)(2,1)}) %reduce-scatter.7.cloned.1.call-update) | async-done | bytes 262160 | tf_op jit(solution)/shard_map/reduce_scatter | solution.py:85
  348.2 41.9 %reduce-scatter.5.cloned.1.call-done = bf16[128,1024]{0,1:T(8,128)(2,1)} async-done(((bf16[128,8192]{0,1:T(8,128)(2,1)}), bf16[128,1024]{0,1:T(8,128)(2,1)}) %reduce-scatter.5.cloned.1.call-update) | async-done | bytes 262160 | tf_op jit(solution)/shard_map/reduce_scatter | solution.py:64
  391.9 45.8 %all-reduce.3.cloned.1.call-done = (bf16[8,128,128]{2,1,0:T(8,128)(2,1)}, bf16[8,128,128]{2,1,0:T(8,128)(2,1)}) async-done(((bf16[8,128,128]{2,1,0:T(8,128)(2,1)}, bf16[8,128,128]{2,1,0:T(8,128)(2,1)}), (bf16[8,128,128]{2,1,0:T(8,128)(2,1)}, bf16[8,128,128]{2,1,0:T(8,128)(2,1)})) %all-reduce.3.cloned.1.call-update) | async-done | bytes 524304 | tf_op jit(solution)/shard_map/psum | solution.py:107
  (81 shorter events, 47.0 us)
Async XLA Ops:
  7.2 27.4 %copy-start = (s32[128,1]{0,1:T(1,128)S(1)}, s32[128,1]{0,1:T(1,128)}, u32[]{:S(2)}) copy-start(s32[128,1]{0,1:T(1,128)} %param.15) | copy-start | bytes 1540
  7.2 85.9 %all-gather.8.cloned.1.call-start = ((), (), s32[]{:S(2)}) async-start(), calls=%async_computation.6 | async-start | bytes 2359296 | tf_op jit(solution)/shard_map/all_gather | solution.py:49
  9.0 96.9 %all-gather.6.cloned.1.call-start = ((), (), s32[]{:S(2)}) async-start(), calls=%async_computation.5 | async-start | bytes 4456448 | tf_op jit(solution)/shard_map/all_gather | solution.py:51
  9.8 138.0 %all-gather.4.cloned.1.call-start = ((), (), s32[]{:S(2)}) async-start(), calls=%async_computation.4 | async-start | bytes 4456448 | tf_op jit(solution)/shard_map/all_gather | solution.py:58
  10.5 275.0 %reduce-scatter.9.cloned.1.call-start = ((), (), s32[]{:S(2)}) async-start(), calls=%async_computation.9 | async-start | bytes 4456448 | tf_op jit(solution)/shard_map/reduce_scatter | solution.py:99
  11.7 12.5 %collective-permute-start = (bf16[128,1024]{0,1:T(8,128)(2,1)S(1)}, bf16[128,1024]{0,1:T(8,128)(2,1)S(1)}, u32[]{:S(2)}, u32[]{:S(2)}) collective-permute-start(bf16[128,1024]{0,1:T(8,128)(2,1)S(1)} %copy.66), channel_id=1, source_target_pairs={{0,1},{1,2},{2,3},{3,4},{4,5},{5,6},{6,7},{7,0},{8,9},{9,10},{10,1... | collective-permute-start | bytes 786440 | tf_op jit(solution)/shard_map/ppermute | solution.py:70
  24.2 9.8 %collective-permute-start.1 = (bf16[128,1024]{0,1:T(8,128)(2,1)S(1)}, bf16[128,1024]{0,1:T(8,128)(2,1)S(1)}, u32[]{:S(2)}, u32[]{:S(2)}) collective-permute-start(bf16[128,1024]{0,1:T(8,128)(2,1)S(1)} %collective-permute-done), channel_id=1, source_target_pairs={{0,1},{1,2},{2,3},{3,4},{4,5},{5,6},{6,7},{7,0},{8,9},{9,10},{10,1... | collective-permute-start | bytes 786440 | tf_op jit(solution)/shard_map/ppermute | solution.py:70
  34.0 12.9 %collective-permute-start.2 = (bf16[128,1024]{0,1:T(8,128)(2,1)S(1)}, bf16[128,1024]{0,1:T(8,128)(2,1)S(1)}, u32[]{:S(2)}, u32[]{:S(2)}) collective-permute-start(bf16[128,1024]{0,1:T(8,128)(2,1)S(1)} %collective-permute-done.1), channel_id=1, source_target_pairs={{0,1},{1,2},{2,3},{3,4},{4,5},{5,6},{6,7},{7,0},{8,9},{9,10},{10,1... | collective-permute-start | bytes 786440 | tf_op jit(solution)/shard_map/ppermute | solution.py:70
  46.9 13.2 %collective-permute-start.3 = (bf16[128,1024]{0,1:T(8,128)(2,1)S(1)}, bf16[128,1024]{0,1:T(8,128)(2,1)S(1)}, u32[]{:S(2)}, u32[]{:S(2)}) collective-permute-start(bf16[128,1024]{0,1:T(8,128)(2,1)S(1)} %collective-permute-done.2), channel_id=1, source_target_pairs={{0,1},{1,2},{2,3},{3,4},{4,5},{5,6},{6,7},{7,0},{8,9},{9,10},{10,1... | collective-permute-start | bytes 786440 | tf_op jit(solution)/shard_map/ppermute | solution.py:70
  60.2 7.0 %collective-permute-start.4 = (bf16[128,1024]{0,1:T(8,128)(2,1)S(1)}, bf16[128,1024]{0,1:T(8,128)(2,1)S(1)}, u32[]{:S(2)}, u32[]{:S(2)}) collective-permute-start(bf16[128,1024]{0,1:T(8,128)(2,1)S(1)} %collective-permute-done.3), channel_id=1, source_target_pairs={{0,1},{1,2},{2,3},{3,4},{4,5},{5,6},{6,7},{7,0},{8,9},{9,10},{10,1... | collective-permute-start | bytes 786440 | tf_op jit(solution)/shard_map/ppermute | solution.py:70
  67.2 8.1 %collective-permute-start.5 = (bf16[128,1024]{0,1:T(8,128)(2,1)S(1)}, bf16[128,1024]{0,1:T(8,128)(2,1)S(1)}, u32[]{:S(2)}, u32[]{:S(2)}) collective-permute-start(bf16[128,1024]{0,1:T(8,128)(2,1)S(1)} %collective-permute-done.4), channel_id=1, source_target_pairs={{0,1},{1,2},{2,3},{3,4},{4,5},{5,6},{6,7},{7,0},{8,9},{9,10},{10,1... | collective-permute-start | bytes 786440 | tf_op jit(solution)/shard_map/ppermute | solution.py:70
  75.2 9.4 %collective-permute-start.6 = (bf16[128,1024]{0,1:T(8,128)(2,1)S(1)}, bf16[128,1024]{0,1:T(8,128)(2,1)S(1)}, u32[]{:S(2)}, u32[]{:S(2)}) collective-permute-start(bf16[128,1024]{0,1:T(8,128)(2,1)S(1)} %collective-permute-done.5), channel_id=1, source_target_pairs={{0,1},{1,2},{2,3},{3,4},{4,5},{5,6},{6,7},{7,0},{8,9},{9,10},{10,1... | collective-permute-start | bytes 786440 | tf_op jit(solution)/shard_map/ppermute | solution.py:70
  153.1 5.0 %copy-start.2 = (bf16[128,128,128]{2,1,0:T(8,128)(2,1)S(1)}, bf16[128,128,128]{2,1,0:T(8,128)(2,1)}, u32[]{:S(2)}) copy-start(bf16[128,128,128]{2,1,0:T(8,128)(2,1)} %gather_fusion.4) | copy-start | bytes 12582916
  166.6 137.9 %reduce-scatter.11.cloned.1.call-start = ((), (), s32[]{:S(2)}) async-start(), calls=%async_computation.10 | async-start | bytes 4456448 | tf_op jit(solution)/shard_map/reduce_scatter | solution.py:102
  183.9 162.5 %reduce-scatter.7.cloned.1.call-start = ((), (), s32[]{:S(2)}) async-start(), calls=%async_computation.8 | async-start | bytes 2359296 | tf_op jit(solution)/shard_map/reduce_scatter | solution.py:85
  234.7 155.4 %reduce-scatter.5.cloned.1.call-start = ((), (), s32[]{:S(2)}) async-start(), calls=%async_computation.7 | async-start | bytes 2359296 | tf_op jit(solution)/shard_map/reduce_scatter | solution.py:64
  279.9 161.3 %copy-start.1 = (s32[128,1]{0,1:T(1,128)S(1)}, s32[128,1]{0,1:T(1,128)}, u32[]{:S(2)}) copy-start(s32[128,1]{0,1:T(1,128)} %param.15) | copy-start | bytes 1540
  285.5 152.2 %all-reduce.3.cloned.1.call-start = ((), (), s32[]{:S(2)}) async-start(), calls=%async_computation.11 | async-start | bytes 1048576 | tf_op jit(solution)/shard_map/psum | solution.py:107
Sparse Core Ops, SparseCore 0:
  10.4 52.7 all-gather.7
  65.1 40.8 all-gather.5
  107.8 39.9 all-gather.3
  166.7 66.5 reduce-scatter.8
  235.8 68.6 reduce-scatter.10
  306.9 39.4 reduce-scatter.6
  349.0 41.0 reduce-scatter.4
  392.7 44.9 all-reduce.2
